TPU v7x, 256 devices: a whole 4x4x8 slice. The times are simulated.
256 devices in a mesh: gz: 8 (over x, core), xy: 32 (over y, z).
Axes of the slice: x: 4, y: 4, z: 8, core: 2. Of those that a mesh axis runs over, the one named last changes fastest.
Arguments:
- x_start: float32 [2, 8, 64, 512, 128], P(None, None, 'gz', 'xy'), may hold values from -6 to 6
- rhs: float32 [2, 8, 64, 512, 128], P(None, None, 'gz', 'xy'), may hold values from -20 to 20
- wave_sq: float32 [64, 512, 128], P('gz', 'xy'), may hold values from 0.3 to 1.5
- damping: float32 [64, 512, 128], P('gz', 'xy'), may hold values from 0.05 to 0.6
- front: float32 [2, 8192, 8192], P(None, ('gz', 'xy')), may hold values from -0.0703125 to 0.0703125
- front_order: int32 [8, 32, 32], P('gz', 'xy'), may hold values from 0 to 31, each once within a row
- pair_count: int32 [8, 32, 32], P('gz'), may hold values from 0 to 3, as said below
- sep_cell: int32 [8, 32, 96], P('gz', 'xy'), may hold values from 0 to 14463, as said below
Outputs:
- solution: float32 [2, 8, 64, 512, 128], P(None, None, 'gz', 'xy')
- new_residual: float32 [2, 8, 64, 512, 128], P(None, None, 'gz', 'xy')
Inputs may be any that keep to these rules, and one draw needn't show every extreme that they name: pair_count[g, o, t] counts the separator cells of brick (g, t) whose front rows belong to owner (g, o). For each g and o exactly one brick has 3, one has 2, 27 have 1 and all others 0, so they sum to 32; which bricks is drawn anew for each owner. `sep_cell`: the 96 entries of one brick are distinct local cell indices of that brick, each on its lowest z plane (z = 0) or its lowest y plane (y = 0). Each row front_order[g, o] is a permutation.
All inputs are finite; a program needn't handle non-finite values.
Results may differ from a plain program's by a relative error of at most 0.00011.
Values sent between devices are 32-bit elements; how exact they have to be, the bound alone decides.
A program may use at most 64 MiB of HBM per device.

v0:
```python
from functools import partial
import jax
import jax.numpy as jnp
from jax import lax
from jax.sharding import PartitionSpec as P


def extended(block, sides, width):
    for axis, dim in sides:
        count = lax.axis_size(axis)
        forward = [(i, i + 1) for i in range(count - 1)]
        backward = [(target, source) for source, target in forward]
        low = lax.ppermute(
            lax.slice_in_dim(block, block.shape[dim] - width, None, axis=dim), axis, forward
        )
        high = lax.ppermute(lax.slice_in_dim(block, 0, width, axis=dim), axis, backward)
        block = jnp.concatenate([low, block, high], axis=dim)
    return block


def apply_operator(padded, wave_sq, damping):
    depth, height, width = wave_sq.shape
    centre = padded[:, :, 1 : depth + 1, 1 : height + 1, 1 : width + 1]
    face_sum = jnp.zeros_like(centre)
    edge_sum = jnp.zeros_like(centre)
    corner_sum = jnp.zeros_like(centre)
    for offset_z in (-1, 0, 1):
        for offset_y in (-1, 0, 1):
            for offset_x in (-1, 0, 1):
                nonzero = abs(offset_z) + abs(offset_y) + abs(offset_x)
                if nonzero == 0:
                    continue
                shifted = padded[
                    :,
                    :,
                    1 + offset_z : 1 + offset_z + depth,
                    1 + offset_y : 1 + offset_y + height,
                    1 + offset_x : 1 + offset_x + width,
                ]
                if nonzero == 1:
                    face_sum = face_sum + shifted
                elif nonzero == 2:
                    edge_sum = edge_sum + shifted
                else:
                    corner_sum = corner_sum + shifted
    negative_laplace = (128.0 * centre - 14.0 * face_sum - 3.0 * edge_sum - corner_sum) / 30.0
    real_part = negative_laplace[0] - wave_sq * (centre[0] - damping * centre[1])
    imag_part = negative_laplace[1] - wave_sq * (centre[1] + damping * centre[0])
    return jnp.stack([real_part, imag_part])


def scale_diagonal(field, wave_sq, damping):
    diag_real = 128.0 / 30.0 - wave_sq
    diag_imag = -wave_sq * damping
    modulus = diag_real * diag_real + diag_imag * diag_imag
    return jnp.stack(
        [
            (field[0] * diag_real + field[1] * diag_imag) / modulus,
            (field[1] * diag_real - field[0] * diag_imag) / modulus,
        ]
    )


def pad_width(field):
    return jnp.pad(field, ((0, 0), (0, 0), (0, 0), (0, 0), (1, 1)))


def extend(field):
    padded = extended(field, (("gz", 2), ("xy", 3)), 1)
    return pad_width(padded)


def local(x_start, rhs, wave_sq, damping, front, front_order, pair_count, sep_cell):
    highest = lax.Precision.HIGHEST
    rhs_count = x_start.shape[1]
    components = 2 * rhs_count
    tiles = pair_count.shape[1]
    rows_own = front_order.shape[2]
    slots = sep_cell.shape[2]
    capacity = slots // tiles
    cell_total = wave_sq.size
    own_index = lax.axis_index("xy")
    residual = rhs - apply_operator(extend(x_start), wave_sq, damping)
    scaled = scale_diagonal(residual, wave_sq, damping)
    counts = pair_count[0]
    offsets = jnp.cumsum(counts, axis=1) - counts
    sep_cells = sep_cell[0, 0]
    slot_ids = jnp.arange(slots, dtype=jnp.int32)
    rank_in = slot_ids % capacity
    owner_of = slot_ids // capacity
    sent_counts = lax.dynamic_index_in_dim(counts, own_index, 1, keepdims=False)
    sent_offsets = lax.dynamic_index_in_dim(offsets, own_index, 1, keepdims=False)
    valid_send = (rank_in < sent_counts[owner_of]).astype(jnp.float32)
    flat_residual = residual.reshape(components, cell_total)
    slot_vals = jnp.take(flat_residual, sep_cells, axis=1) * valid_send[None, :]
    got_counts = lax.dynamic_index_in_dim(counts, own_index, 0, keepdims=False)
    got_offsets = lax.dynamic_index_in_dim(offsets, own_index, 0, keepdims=False)
    entry = got_offsets[owner_of] + rank_in
    valid_got = rank_in < got_counts[owner_of]
    row_ids = jnp.arange(rows_own, dtype=jnp.int32)
    entry_map = (valid_got[:, None] & (entry[:, None] == row_ids[None, :])).astype(jnp.float32)
    order_map = (front_order[0, 0][:, None] == row_ids[None, :]).astype(jnp.float32)
    all_slots = lax.all_gather(slot_vals, "xy", axis=1, tiled=True)
    received = lax.dynamic_index_in_dim(
        all_slots.reshape(components, tiles, tiles, capacity), own_index, 2, keepdims=False
    ).reshape(components, slots)
    by_entry = jnp.dot(received, entry_map, precision=highest, preferred_element_type=jnp.float32)
    owned = jnp.dot(by_entry, order_map, precision=highest, preferred_element_type=jnp.float32)
    front_real = front[0]
    front_imag = front[1]
    product = partial(
        lax.dot_general,
        dimension_numbers=(((1,), (1,)), ((), ())),
        precision=highest,
        preferred_element_type=jnp.float32,
    )
    blank = jnp.zeros((rows_own, rhs_count), jnp.float32)
    part_vals = lax.all_gather(owned, ("gz", "xy"), axis=1, tiled=True)
    vals_real = part_vals[:rhs_count]
    vals_imag = part_vals[rhs_count:]
    new_real = blank + product(front_real, vals_real) - product(front_imag, vals_imag)
    new_imag = blank + product(front_real, vals_imag) + product(front_imag, vals_real)
    solved = jnp.concatenate([new_real.T, new_imag.T], axis=0)
    solved_entry = jnp.dot(
        solved, order_map.T, precision=highest, preferred_element_type=jnp.float32
    )
    owner_rows = lax.all_gather(solved_entry, "xy", axis=1, tiled=True)
    pick = jnp.minimum(owner_of * rows_own + sent_offsets[owner_of] + rank_in, tiles * rows_own - 1)
    returned = jnp.take(owner_rows, pick, axis=1) * valid_send[None, :]
    correction = (
        jnp.zeros((components, cell_total), jnp.float32)
        .at[:, sep_cells]
        .add(returned)
        .reshape(residual.shape)
    )
    direction = scaled + correction
    image = apply_operator(extend(direction), wave_sq, damping)
    num_real = jnp.sum(image[0] * residual[0] + image[1] * residual[1], axis=(1, 2, 3))
    num_imag = jnp.sum(image[0] * residual[1] - image[1] * residual[0], axis=(1, 2, 3))
    den_part = jnp.sum(image[0] * image[0] + image[1] * image[1], axis=(1, 2, 3))
    totals = lax.psum(jnp.stack([num_real, num_imag, den_part]), ("gz", "xy"))
    denom = totals[2] + 1e-06
    alpha_real = (totals[0] / denom)[:, None, None, None]
    alpha_imag = (totals[1] / denom)[:, None, None, None]
    solution = jnp.stack(
        [
            x_start[0] + alpha_real * direction[0] - alpha_imag * direction[1],
            x_start[1] + alpha_real * direction[1] + alpha_imag * direction[0],
        ]
    )
    new_residual = jnp.stack(
        [
            residual[0] - alpha_real * image[0] + alpha_imag * image[1],
            residual[1] - alpha_real * image[1] - alpha_imag * image[0],
        ]
    )
    return (solution, new_residual)


def solution(mesh):
    in_specs = (
        P(None, None, "gz", "xy", None),
        P(None, None, "gz", "xy", None),
        P("gz", "xy", None),
        P("gz", "xy", None),
        P(None, ("gz", "xy"), None),
        P("gz", "xy", None),
        P("gz", None, None),
        P("gz", "xy", None),
    )
    out_specs = (P(None, None, "gz", "xy", None), P(None, None, "gz", "xy", None))
    return jax.shard_map(local, mesh=mesh, in_specs=in_specs, out_specs=out_specs, check_vma=False)
```

profile of v0, /device:TPU:1, one launch (start us, length us, event | category | flops | bytes accessed | tf_op | source)
XLA Modules:
  0.0 355.8 jit_solution(13634245641871823886)
XLA Ops:
  0.7 1.1 fusion.91
  1.8 4.5 %collective-permute-start = (f32[2,8,1,16,128]{4,3,2,1,0:T(8,128)S(1)}, f32[2,8,1,16,128]{4,3,2,1,0:T(8,128)S(1)}, u32[]{:S(2)}, u32[]{:S(2)}) collective-permute-start(f32[2,8,1,16,128]{4,3,2,1,0:T(8,128)S(1)} %get-tuple-element.29), channel_id=1, source_target_pairs={{0,32},{32,64},{64,96},{96,128},{128,160},{160,192},{192,224},{1,3... | collective-permute-start | bytes 393224 | tf_op jit(solution)/shard_map/ppermute | solution.py:13
  6.3 1.9 collective-permute-start.1
  8.2 0.9 dynamic-slice_reduce_fusion
  9.1 0.7 fusion.78
  9.8 0.9 reduce_window_sum.11
  10.7 0.7 bitcast_subtract_fusion.1
  11.6 1.2 gather_fusion
  13.6 1.2 gather_fusion.2
  14.8 0.7 compare_convert_fusion
  15.5 1.2 gather_fusion.4
  16.7 1.2 gather_fusion.3
  18.0 0.7 multiply_add_fusion.2
  19.0 3.5 collective-permute-start.2
  22.6 1.3 collective-permute-start.3
  24.0 3.9 %collective-permute-done.3 = f32[2,8,10,1,128]{4,3,2,1,0:T(1,128)S(1)} collective-permute-done((f32[2,8,10,1,128]{4,3,2,1,0:T(1,128)S(1)}, f32[2,8,10,1,128]{4,3,2,1,0:T(1,128)S(1)}, u32[]{:S(2)}, u32[]{:S(2)}) %collective-permute-start.3) | collective-permute-done | bytes 81952 | tf_op jit(solution)/shard_map/ppermute | solution.py:16
  28.6 1.8 select_maximum_fusion.4
  30.3 5.6 %fusion.16 = f32[2,8,8,16,128]{4,3,2,1,0:T(8,128)} fusion(f32[2,8,10,16,128]{4,3,2,1,0:T(8,128)S(1)} %constant_dynamic-update-slice_fusion, f32[2,8,10,1,128]{4,3,2,1,0:T(1,128)} %copy-done.6, f32[2,8,10,1,128]{4,3,2,1,0:T(1,128)} %copy-done.5, f32[2,8,10,18,130]{4,3,2,1,0:T(8,128)S(1)} %select_maximum_fusion.4, ...), kind=kLoop, calls=%fused_computation.45 | loop fusion | flops 9961472 | bytes 22708224 | tf_op jit(solution)/shard_map/div | solution.py:46
  35.9 1.5 slice_subtract_fusion.1
  37.8 4.6 %copy.23 = f32[16,16384]{0,1:T(8,128)} copy(f32[16,16384]{1,0:T(8,128)S(1)} %reshape.193) | data formatting | bytes 2097152 | tf_op jit(solution)/shard_map/reshape | solution.py:94
  42.4 4.0 %gather_fusion.1 = f32[96,16]{1,0:T(8,128)S(1)} fusion(f32[16,16384]{0,1:T(8,128)} %copy.23, s32[1024]{0:T(1024)S(1)} %pad_clamp_fusion.1), kind=kCustom, calls=%fused_computation.1 | custom fusion | bytes 12672 | tf_op jit(solution)/shard_map/jit(_take)/gather | solution.py:95
  46.6 40.5 %all-gather = f32[32,96,16]{1,2,0:T(8,128)S(1)} all-gather(f32[1,96,16]{1,2,0:T(8,128)S(1)} %copy.24), channel_id=1, replica_groups=mesh['gz'=8,'xy'=32] {'xy'}, dimensions={0}, use_global_device_ids=true | all-gather | bytes 202752 | tf_op jit(solution)/shard_map/all_gather | solution.py:103
  87.8 1.7 reshape.194
  89.6 0.9 constant_dynamic-slice_fusion.2
  90.9 81.8 %all-gather.1 = f32[256,32,16]{1,2,0:T(8,128)S(1)} all-gather(f32[1,32,16]{1,2,0:T(8,128)S(1)} %convolution_bitcast_fusion.1), channel_id=1, replica_groups=mesh['gz'=8,'xy'=32] {'gz','xy'}, dimensions={0}, use_global_device_ids=true | all-gather | bytes 526336 | tf_op jit(solution)/shard_map/all_gather | solution.py:118
  172.7 2.0 copy.27
  174.7 2.5 reshape.256
  177.3 2.3 fusion.40
  179.6 2.2 fusion.38
  181.7 0.9 convolution_subtract_fusion
  182.7 1.0 convolution_add_fusion
  183.8 36.2 %all-gather.2 = f32[32,32,16]{1,2,0:T(8,128)S(1)} all-gather(f32[1,32,16]{1,2,0:T(8,128)S(1)} %convolution_bitcast_fusion), channel_id=1, replica_groups=mesh['gz'=8,'xy'=32] {'xy'}, dimensions={0}, use_global_device_ids=true | all-gather | bytes 67584 | tf_op jit(solution)/shard_map/all_gather | solution.py:127
  220.2 5.0 %scatter_custom_fusion = f32[16,16384]{0,1:T(8,128)} fusion(s32[96]{0:T(128)S(1)} %fusion.80, f32[]{:T(128)} %constant.81.clone.1, f32[96]{0:T(128)S(1)} %get-tuple-element.33, f32[]{:T(128)} %constant.96.clone.1, pred[96]{0:T(512)(128)(4,1)S(1)} %compare_and_fusion.1, f32[16,1024]{0,1:T(8,128)S(1)} %bitcast.110, s32[1024]{0:T(1024)S(1)} %pad_clamp_fusion), kind=kCustom, calls=%fused_computation.9 | custom fusion | flops 4608 | bytes 1577992 | tf_op jit(solution)/shard_map/scatter-add | solution.py:133
  225.2 5.1 %copy.30 = f32[16,16384]{1,0:T(8,128)S(1)} copy(f32[16,16384]{0,1:T(8,128)} %scatter_custom_fusion) | data formatting | bytes 2097152 | tf_op jit(solution)/shard_map/scatter-add | solution.py:133
  231.6 15.0 %collective-permute-start.4 = (f32[2,8,1,16,128]{4,3,2,1,0:T(8,128)S(1)}, f32[2,8,1,16,128]{4,3,2,1,0:T(8,128)S(1)}, u32[]{:S(2)}, u32[]{:S(2)}) collective-permute-start(f32[2,8,1,16,128]{4,3,2,1,0:T(8,128)S(1)} %get-tuple-element.26), channel_id=1, source_target_pairs={{0,32},{32,64},{64,96},{96,128},{128,160},{160,192},{192,224},{1,3... | collective-permute-start | bytes 393224 | tf_op jit(solution)/shard_map/ppermute | solution.py:13
  246.6 3.0 collective-permute-start.5
  249.6 3.3 collective-permute-done.5
  253.0 3.0 collective-permute-start.6
  256.0 1.5 collective-permute-start.7
  257.5 3.7 %collective-permute-done.7 = f32[2,8,10,1,128]{4,3,2,1,0:T(1,128)S(1)} collective-permute-done((f32[2,8,10,1,128]{4,3,2,1,0:T(1,128)S(1)}, f32[2,8,10,1,128]{4,3,2,1,0:T(1,128)S(1)}, u32[]{:S(2)}, u32[]{:S(2)}) %collective-permute-start.7) | collective-permute-done | bytes 81952 | tf_op jit(solution)/shard_map/ppermute | solution.py:16
  261.2 2.3 maximum_maximum_fusion
  263.5 2.7 select_maximum_fusion
  266.2 6.5 %fusion.30 = f32[2,8,8,16,128]{4,3,2,1,0:T(8,128)} fusion(f32[2,8,10,18,130]{4,3,2,1,0:T(8,128)S(1)} %select_maximum_fusion, f32[2,8,10,17,128]{4,3,2,1,0:T(8,128)} %get-tuple-element.17, f32[2,8,10,17,128]{4,3,2,1,0:T(8,128)} %get-tuple-element.16, f32[2,8,1,16,128]{4,3,2,1,0:T(8,128)S(1)} %collective-permute-done.5, ...), kind=kLoop, calls=%fused_computation.60 | loop fusion | flops 8388608 | bytes 27525120 | tf_op jit(solution)/shard_map/div | solution.py:46
  272.7 1.4 fusion.52
  274.4 77.1 %psum.7 = f32[3,8]{1,0:T(4,128)S(1)} all-reduce(f32[3,8]{1,0:T(4,128)S(1)} %pad_maximum_fusion.12), channel_id=1, replica_groups=mesh['gz'=8,'xy'=32] {'gz','xy'}, use_global_device_ids=true, to_apply=%region_5.6 | all-reduce | flops 24 | bytes 192 | tf_op jit(solution)/shard_map/psum | solution.py:141
  351.5 2.0 multiply_add_fusion
  353.7 1.0 pad_maximum_fusion.8
  354.8 1.0 pad_maximum_fusion.7
  (63 shorter events, 6.0 us)
Async XLA Ops:
  0.6 18.1 %copy-start = (f32[2,8,8,16,128]{4,3,2,1,0:T(8,128)S(1)}, f32[2,8,8,16,128]{4,3,2,1,0:T(8,128)}, u32[]{:S(2)}) copy-start(f32[2,8,8,16,128]{4,3,2,1,0:T(8,128)} %param.8) | copy-start | bytes 3145732
  0.6 17.3 %copy-start.3 = (f32[8,16,128]{2,1,0:T(8,128)S(1)}, f32[8,16,128]{2,1,0:T(8,128)}, u32[]{:S(2)}) copy-start(f32[8,16,128]{2,1,0:T(8,128)} %param.10) | copy-start | bytes 196612
  0.7 17.3 %copy-start.2 = (f32[8,16,128]{2,1,0:T(8,128)S(1)}, f32[8,16,128]{2,1,0:T(8,128)}, u32[]{:S(2)}) copy-start(f32[8,16,128]{2,1,0:T(8,128)} %param.11) | copy-start | bytes 196612
  1.8 17.0 %collective-permute-start = (f32[2,8,1,16,128]{4,3,2,1,0:T(8,128)S(1)}, f32[2,8,1,16,128]{4,3,2,1,0:T(8,128)S(1)}, u32[]{:S(2)}, u32[]{:S(2)}) collective-permute-start(f32[2,8,1,16,128]{4,3,2,1,0:T(8,128)S(1)} %get-tuple-element.29), channel_id=1, source_target_pairs={{0,32},{32,64},{64,96},{96,128},{128,160},{160,192},{192,224},{1,3... | collective-permute-start | bytes 393224 | tf_op jit(solution)/shard_map/ppermute | solution.py:13
  6.3 12.6 %collective-permute-start.1 = (f32[2,8,1,16,128]{4,3,2,1,0:T(8,128)S(1)}, f32[2,8,1,16,128]{4,3,2,1,0:T(8,128)S(1)}, u32[]{:S(2)}, u32[]{:S(2)}) collective-permute-start(f32[2,8,1,16,128]{4,3,2,1,0:T(8,128)S(1)} %get-tuple-element.28), channel_id=1, source_target_pairs={{32,0},{64,32},{96,64},{128,96},{160,128},{192,160},{224,192},{33,... | collective-permute-start | bytes 393224 | tf_op jit(solution)/shard_map/ppermute | solution.py:16
  19.0 5.0 %collective-permute-start.2 = (f32[2,8,10,1,128]{4,3,2,1,0:T(1,128)S(1)}, f32[2,8,10,1,128]{4,3,2,1,0:T(1,128)S(1)}, u32[]{:S(2)}, u32[]{:S(2)}) collective-permute-start(f32[2,8,10,1,128]{4,3,2,1,0:T(1,128)S(1)} %get-tuple-element.20), channel_id=1, source_target_pairs={{0,1},{1,2},{2,3},{3,4},{4,5},{5,6},{6,7},{7,8},{8,9},{9,10},{10,1... | collective-permute-start | bytes 245768 | tf_op jit(solution)/shard_map/ppermute | solution.py:13
  22.6 5.4 %collective-permute-start.3 = (f32[2,8,10,1,128]{4,3,2,1,0:T(1,128)S(1)}, f32[2,8,10,1,128]{4,3,2,1,0:T(1,128)S(1)}, u32[]{:S(2)}, u32[]{:S(2)}) collective-permute-start(f32[2,8,10,1,128]{4,3,2,1,0:T(1,128)S(1)} %get-tuple-element.21), channel_id=1, source_target_pairs={{1,0},{2,1},{3,2},{4,3},{5,4},{6,5},{7,6},{8,7},{9,8},{10,9},{11,1... | collective-permute-start | bytes 245768 | tf_op jit(solution)/shard_map/ppermute | solution.py:16
  24.0 3.9 %copy-start.5 = (f32[2,8,10,1,128]{4,3,2,1,0:T(1,128)}, f32[2,8,10,1,128]{4,3,2,1,0:T(1,128)S(1)}, u32[]{:S(2)}) copy-start(f32[2,8,10,1,128]{4,3,2,1,0:T(1,128)S(1)} %collective-permute-done.2) | copy-start | bytes 245764
  27.9 0.6 copy-start.6
  35.9 1.5 copy-start.4
  87.8 2.9 copy-start.10
  177.3 4.5 %copy-start.1 = (f32[2,32,8192]{2,1,0:T(8,128)S(1)}, f32[2,32,8192]{2,1,0:T(8,128)}, u32[]{:S(2)}) copy-start(f32[2,32,8192]{2,1,0:T(8,128)} %param.12) | copy-start | bytes 6291460
  230.3 0.9 copy-start.7
  230.3 0.9 copy-start.8
  230.3 0.9 copy-start.9
  231.6 18.0 %collective-permute-start.4 = (f32[2,8,1,16,128]{4,3,2,1,0:T(8,128)S(1)}, f32[2,8,1,16,128]{4,3,2,1,0:T(8,128)S(1)}, u32[]{:S(2)}, u32[]{:S(2)}) collective-permute-start(f32[2,8,1,16,128]{4,3,2,1,0:T(8,128)S(1)} %get-tuple-element.26), channel_id=1, source_target_pairs={{0,32},{32,64},{64,96},{96,128},{128,160},{160,192},{192,224},{1,3... | collective-permute-start | bytes 393224 | tf_op jit(solution)/shard_map/ppermute | solution.py:13
  246.6 6.3 %collective-permute-start.5 = (f32[2,8,1,16,128]{4,3,2,1,0:T(8,128)S(1)}, f32[2,8,1,16,128]{4,3,2,1,0:T(8,128)S(1)}, u32[]{:S(2)}, u32[]{:S(2)}) collective-permute-start(f32[2,8,1,16,128]{4,3,2,1,0:T(8,128)S(1)} %get-tuple-element.27), channel_id=1, source_target_pairs={{32,0},{64,32},{96,64},{128,96},{160,128},{192,160},{224,192},{33,... | collective-permute-start | bytes 393224 | tf_op jit(solution)/shard_map/ppermute | solution.py:16
  253.0 4.5 %collective-permute-start.6 = (f32[2,8,10,1,128]{4,3,2,1,0:T(1,128)S(1)}, f32[2,8,10,1,128]{4,3,2,1,0:T(1,128)S(1)}, u32[]{:S(2)}, u32[]{:S(2)}) collective-permute-start(f32[2,8,10,1,128]{4,3,2,1,0:T(1,128)S(1)} %get-tuple-element.18), channel_id=1, source_target_pairs={{0,1},{1,2},{2,3},{3,4},{4,5},{5,6},{6,7},{7,8},{8,9},{9,10},{10,1... | collective-permute-start | bytes 245768 | tf_op jit(solution)/shard_map/ppermute | solution.py:13
  256.0 5.2 %collective-permute-start.7 = (f32[2,8,10,1,128]{4,3,2,1,0:T(1,128)S(1)}, f32[2,8,10,1,128]{4,3,2,1,0:T(1,128)S(1)}, u32[]{:S(2)}, u32[]{:S(2)}) collective-permute-start(f32[2,8,10,1,128]{4,3,2,1,0:T(1,128)S(1)} %get-tuple-element.19), channel_id=1, source_target_pairs={{1,0},{2,1},{3,2},{4,3},{5,4},{6,5},{7,6},{8,7},{9,8},{10,9},{11,1... | collective-permute-start | bytes 245768 | tf_op jit(solution)/shard_map/ppermute | solution.py:16
where the time goes:
time: 357 us; the launch traced here: 356 us
  blocking collectives  236 us (66%)
  other arithmetic  35.8 us (10%)
  starting transfers between devices  33.7 us (9%)
  local copies, waits for them, and re-layouts  31.7 us (9%)
  waiting for transfers between devices  11 us (3%)
  matrix products  6.99 us (2%)
    all_gather x1, blocking collectives, local(): part_vals = lax.all_gather(owned, ('gz', 'xy'), axis=1, tiled=True)  81.8 us
    psum x1, blocking collectives, local(): totals = lax.psum(jnp.stack([num_real, num_imag, den_part]), ('gz', 'xy'))  77.1 us
    all_gather x1, blocking collectives, local(): all_slots = lax.all_gather(slot_vals, 'xy', axis=1, tiled=True)  40.5 us
    all_gather x1, blocking collectives, local(): owner_rows = lax.all_gather(solved_entry, 'xy', axis=1, tiled=True)  36.2 us
    ppermute x4, starting transfers between devices, extended(): lax.ppermute(lax.slice_in_dim(block, block.shape[dim] - width, None, axis...  26 us
    div x2, other arithmetic, apply_operator(): (128.0 * centre - 14.0 * face_sum - 3.0 * edge_sum - corner_sum) / 30.0  12 us
    ppermute x4, waiting for transfers between devices, extended(): lax.ppermute(lax.slice_in_dim(block, 0, width, axis=dim), axis, backward)  10.9 us
    ppermute x4, starting transfers between devices, extended(): lax.ppermute(lax.slice_in_dim(block, 0, width, axis=dim), axis, backward)  7.72 us
  transfers between devices with their start and end apart: 8, of which 4 were waited for; matrix products, arithmetic and copies ran while one was open for 3% of the time, Pallas kernels for 0%

commit v1 on v0

--- a/solution.py
+++ b/solution.py
@@ -115,7 +115,9 @@
         preferred_element_type=jnp.float32,
     )
     blank = jnp.zeros((rows_own, rhs_count), jnp.float32)
-    part_vals = lax.all_gather(owned, ("gz", "xy"), axis=1, tiled=True)
+    part_vals = jnp.concatenate(
+        lax.all_to_all(jnp.stack([owned] * lax.axis_size(("gz", "xy"))), ("gz", "xy"), 0, 0), axis=1
+    )
     vals_real = part_vals[:rhs_count]
     vals_imag = part_vals[rhs_count:]
     new_real = blank + product(front_real, vals_real) - product(front_imag, vals_imag)

time: 357 us -> 327 us (0.916)
  blocking collectives: 236 us -> 152 us
  starting transfers between devices: 33.7 us -> 56.3 us
  waiting for transfers between devices: 11 us -> 32.4 us
  local copies, waits for them, and re-layouts: 31.7 us -> 39.6 us
    all_gather x1 -> x0, blocking collectives: 81.8 us -> none  [local(): part_vals = lax.all_gather(owned, ('gz', 'xy'), axis=1, tiled=True)]
    all_to_all x0 -> x1, starting transfers between devices: none -> 24.1 us  [local(): lax.all_to_all(jnp.stack([owned] * lax.axis_size(('gz', 'xy'))), ('gz', '...]
    all_to_all x0 -> x1, waiting for transfers between devices: none -> 20.3 us  [local(): lax.all_to_all(jnp.stack([owned] * lax.axis_size(('gz', 'xy'))), ('gz', '...]
    slice x0 -> x5, local copies, waits for them, and re-layouts: none -> 5.26 us  [the longest x3 3.34 us: local(): vals_real = part_vals[:rhs_count]]
    unnamed x30 -> x27, local copies, waits for them, and re-layouts: 5.13 us -> 7.77 us
  transfers between devices with their start and end apart: 8 -> 9, of which waited for: 4 -> 5; matrix products, arithmetic and copies ran while one was open for 3% -> 3% of each run, Pallas kernels for 0% -> 0%
where the time goes in v1:
time: 327 us; the launch traced here: 326 us
  blocking collectives  152 us (46%)
  starting transfers between devices  56.3 us (17%)
  local copies, waits for them, and re-layouts  39.6 us (12%)
  other arithmetic  37.8 us (12%)
  waiting for transfers between devices  32.4 us (10%)
  matrix products  6.99 us (2%)
    psum x1, blocking collectives, local(): totals = lax.psum(jnp.stack([num_real, num_imag, den_part]), ('gz', 'xy'))  76.9 us
    all_gather x1, blocking collectives, local(): all_slots = lax.all_gather(slot_vals, 'xy', axis=1, tiled=True)  40.5 us
    all_gather x1, blocking collectives, local(): owner_rows = lax.all_gather(solved_entry, 'xy', axis=1, tiled=True)  34.7 us
    ppermute x4, starting transfers between devices, extended(): lax.ppermute(lax.slice_in_dim(block, block.shape[dim] - width, None, axis...  25.6 us
    all_to_all x1, starting transfers between devices, local(): lax.all_to_all(jnp.stack([owned] * lax.axis_size(('gz', 'xy'))), ('gz', '...  24.1 us
    all_to_all x1, waiting for transfers between devices, local(): lax.all_to_all(jnp.stack([owned] * lax.axis_size(('gz', 'xy'))), ('gz', '...  20.3 us
    div x2, other arithmetic, apply_operator(): (128.0 * centre - 14.0 * face_sum - 3.0 * edge_sum - corner_sum) / 30.0  12.1 us
    ppermute x4, waiting for transfers between devices, extended(): lax.ppermute(lax.slice_in_dim(block, 0, width, axis=dim), axis, backward)  11.9 us
  transfers between devices with their start and end apart: 9, of which 5 were waited for; matrix products, arithmetic and copies ran while one was open for 3% of the time, Pallas kernels for 0%

profile of v1, /device:TPU:1, one launch (start us, length us, event | category | flops | bytes accessed | tf_op | source)
XLA Modules:
  0.0 326.2 jit_solution(17908235273276215462)
XLA Ops:
  0.6 1.1 fusion.89
  1.7 4.5 %collective-permute-start = (f32[2,8,1,16,128]{4,3,2,1,0:T(8,128)S(1)}, f32[2,8,1,16,128]{4,3,2,1,0:T(8,128)S(1)}, u32[]{:S(2)}, u32[]{:S(2)}) collective-permute-start(f32[2,8,1,16,128]{4,3,2,1,0:T(8,128)S(1)} %get-tuple-element.31), channel_id=1, source_target_pairs={{0,32},{32,64},{64,96},{96,128},{128,160},{160,192},{192,224},{1,3... | collective-permute-start | bytes 393224 | tf_op jit(solution)/shard_map/ppermute | solution.py:13
  6.2 1.9 collective-permute-start.1
  9.8 0.9 reduce_window_sum.11
  12.3 1.2 gather_fusion.2
  14.2 1.2 gather_fusion.4
  15.4 1.2 gather_fusion.3
  16.7 1.2 gather_fusion
  18.2 3.5 %collective-permute-start.2 = (f32[2,8,10,1,128]{4,3,2,1,0:T(1,128)S(1)}, f32[2,8,10,1,128]{4,3,2,1,0:T(1,128)S(1)}, u32[]{:S(2)}, u32[]{:S(2)}) collective-permute-start(f32[2,8,10,1,128]{4,3,2,1,0:T(1,128)S(1)} %get-tuple-element.22), channel_id=1, source_target_pairs={{0,1},{1,2},{2,3},{3,4},{4,5},{5,6},{6,7},{7,8},{8,9},{9,10},{10,1... | collective-permute-start | bytes 245768 | tf_op jit(solution)/shard_map/ppermute | solution.py:13
  21.8 1.3 collective-permute-start.3
  23.2 3.9 %collective-permute-done.3 = f32[2,8,10,1,128]{4,3,2,1,0:T(1,128)S(1)} collective-permute-done((f32[2,8,10,1,128]{4,3,2,1,0:T(1,128)S(1)}, f32[2,8,10,1,128]{4,3,2,1,0:T(1,128)S(1)}, u32[]{:S(2)}, u32[]{:S(2)}) %collective-permute-start.3) | collective-permute-done | bytes 81952 | tf_op jit(solution)/shard_map/ppermute | solution.py:16
  27.8 1.8 select_maximum_fusion.4
  29.6 5.7 %fusion.16 = f32[2,8,8,16,128]{4,3,2,1,0:T(8,128)} fusion(f32[2,8,10,16,128]{4,3,2,1,0:T(8,128)S(1)} %constant_dynamic-update-slice_fusion, f32[2,8,10,1,128]{4,3,2,1,0:T(1,128)} %copy-done.7, f32[2,8,10,1,128]{4,3,2,1,0:T(1,128)} %copy-done.6, f32[2,8,10,18,130]{4,3,2,1,0:T(8,128)S(1)} %select_maximum_fusion.4, ...), kind=kLoop, calls=%fused_computation.44 | loop fusion | flops 9961472 | bytes 22708224 | tf_op jit(solution)/shard_map/div | solution.py:46
  35.2 1.5 slice_subtract_fusion.1
  37.1 4.6 %copy.23 = f32[16,16384]{0,1:T(8,128)} copy(f32[16,16384]{1,0:T(8,128)S(1)} %reshape.201) | data formatting | bytes 2097152 | tf_op jit(solution)/shard_map/reshape | solution.py:94
  41.7 4.0 %gather_fusion.1 = f32[96,16]{1,0:T(8,128)S(1)} fusion(f32[16,16384]{0,1:T(8,128)} %copy.23, s32[1024]{0:T(1024)S(1)} %pad_clamp_fusion.1), kind=kCustom, calls=%fused_computation.1 | custom fusion | bytes 12672 | tf_op jit(solution)/shard_map/jit(_take)/gather | solution.py:95
  45.9 40.5 %all-gather = f32[32,96,16]{1,2,0:T(8,128)S(1)} all-gather(f32[1,96,16]{1,2,0:T(8,128)S(1)} %copy.24), channel_id=1, replica_groups=mesh['gz'=8,'xy'=32] {'xy'}, dimensions={0}, use_global_device_ids=true | all-gather | bytes 202752 | tf_op jit(solution)/shard_map/all_gather | solution.py:103
  87.1 1.7 reshape.202
  90.2 1.5 stack.20
  91.7 3.1 reshape.278
  94.9 24.1 %all-to-all-start = ((f32[256,1,512]{2,1,0:T(1,128)}), f32[256,1,512]{2,1,0:T(1,128)S(1)}, u32[]{:S(2)}, u32[]{:S(2)}) async-start(f32[256,1,512]{2,1,0:T(1,128)} %reshape.278), calls=%async_computation | async-start | bytes 1048576 | tf_op jit(solution)/shard_map/all_to_all | solution.py:119
  119.0 1.0 add_divide_fusion
  120.0 20.3 %all-to-all-done = f32[256,1,512]{2,1,0:T(1,128)S(1)} async-done(((f32[256,1,512]{2,1,0:T(1,128)}), f32[256,1,512]{2,1,0:T(1,128)S(1)}, u32[]{:S(2)}, u32[]{:S(2)}) %all-to-all-start) | async-done | bytes 524320 | tf_op jit(solution)/shard_map/all_to_all | solution.py:119
  140.8 1.9 reduce.4
  142.7 1.9 reshape.279
  144.6 2.6 fusion.86
  147.9 1.4 copy.28
  149.8 2.3 fusion.40
  152.1 2.2 fusion.38
  154.3 0.9 convolution_subtract_fusion
  155.2 1.0 convolution_add_fusion
  156.4 34.7 %all-gather.1 = f32[32,32,16]{1,2,0:T(8,128)S(1)} all-gather(f32[1,32,16]{1,2,0:T(8,128)S(1)} %convolution_bitcast_fusion), channel_id=1, replica_groups=mesh['gz'=8,'xy'=32] {'xy'}, dimensions={0}, use_global_device_ids=true | all-gather | bytes 67584 | tf_op jit(solution)/shard_map/all_gather | solution.py:129
  191.3 5.0 %scatter_custom_fusion = f32[16,16384]{0,1:T(8,128)} fusion(s32[96]{0:T(128)S(1)} %fusion.77, f32[]{:T(128)} %constant.81.clone.1, f32[96]{0:T(128)S(1)} %get-tuple-element.35, f32[]{:T(128)} %constant.96.clone.1, pred[96]{0:T(512)(128)(4,1)S(1)} %compare_and_fusion.1, f32[16,1024]{0,1:T(8,128)S(1)} %bitcast.107, s32[1024]{0:T(1024)S(1)} %pad_clamp_fusion), kind=kCustom, calls=%fused_computation.9 | custom fusion | flops 4608 | bytes 1577992 | tf_op jit(solution)/shard_map/scatter-add | solution.py:135
  196.3 5.1 %copy.31 = f32[16,16384]{1,0:T(8,128)S(1)} copy(f32[16,16384]{0,1:T(8,128)} %scatter_custom_fusion) | data formatting | bytes 2097152 | tf_op jit(solution)/shard_map/scatter-add | solution.py:135
  202.6 14.5 %collective-permute-start.4 = (f32[2,8,1,16,128]{4,3,2,1,0:T(8,128)S(1)}, f32[2,8,1,16,128]{4,3,2,1,0:T(8,128)S(1)}, u32[]{:S(2)}, u32[]{:S(2)}) collective-permute-start(f32[2,8,1,16,128]{4,3,2,1,0:T(8,128)S(1)} %get-tuple-element.28), channel_id=1, source_target_pairs={{0,32},{32,64},{64,96},{96,128},{128,160},{160,192},{192,224},{1,3... | collective-permute-start | bytes 393224 | tf_op jit(solution)/shard_map/ppermute | solution.py:13
  217.1 1.9 collective-permute-start.5
  219.1 4.3 %collective-permute-done.5 = f32[2,8,1,16,128]{4,3,2,1,0:T(8,128)S(1)} collective-permute-done((f32[2,8,1,16,128]{4,3,2,1,0:T(8,128)S(1)}, f32[2,8,1,16,128]{4,3,2,1,0:T(8,128)S(1)}, u32[]{:S(2)}, u32[]{:S(2)}) %collective-permute-start.5) | collective-permute-done | bytes 131104 | tf_op jit(solution)/shard_map/ppermute | solution.py:16
  223.5 3.0 collective-permute-start.6
  226.6 1.5 collective-permute-start.7
  228.1 3.7 %collective-permute-done.7 = f32[2,8,10,1,128]{4,3,2,1,0:T(1,128)S(1)} collective-permute-done((f32[2,8,10,1,128]{4,3,2,1,0:T(1,128)S(1)}, f32[2,8,10,1,128]{4,3,2,1,0:T(1,128)S(1)}, u32[]{:S(2)}, u32[]{:S(2)}) %collective-permute-start.7) | collective-permute-done | bytes 81952 | tf_op jit(solution)/shard_map/ppermute | solution.py:16
  231.8 2.3 maximum_maximum_fusion
  234.0 2.7 select_maximum_fusion
  236.7 6.4 %fusion.30 = f32[2,8,8,16,128]{4,3,2,1,0:T(8,128)} fusion(f32[2,8,10,18,130]{4,3,2,1,0:T(8,128)S(1)} %select_maximum_fusion, f32[2,8,10,17,128]{4,3,2,1,0:T(8,128)} %get-tuple-element.19, f32[2,8,10,17,128]{4,3,2,1,0:T(8,128)} %get-tuple-element.18, f32[2,8,1,16,128]{4,3,2,1,0:T(8,128)S(1)} %collective-permute-done.5, ...), kind=kLoop, calls=%fused_computation.59 | loop fusion | flops 8388608 | bytes 27525120 | tf_op jit(solution)/shard_map/div | solution.py:46
  243.2 1.4 fusion.52
  245.0 76.9 %psum.7 = f32[3,8]{1,0:T(4,128)S(1)} all-reduce(f32[3,8]{1,0:T(4,128)S(1)} %pad_maximum_fusion.12), channel_id=1, replica_groups=mesh['gz'=8,'xy'=32] {'gz','xy'}, use_global_device_ids=true, to_apply=%region_5.6 | all-reduce | flops 24 | bytes 192 | tf_op jit(solution)/shard_map/psum | solution.py:143
  321.9 2.0 multiply_add_fusion
  324.1 1.0 pad_maximum_fusion.8
  325.2 1.0 pad_maximum_fusion.7
  (68 shorter events, 11.6 us)
Async XLA Ops:
  0.6 17.3 %copy-start = (f32[2,8,8,16,128]{4,3,2,1,0:T(8,128)S(1)}, f32[2,8,8,16,128]{4,3,2,1,0:T(8,128)}, u32[]{:S(2)}) copy-start(f32[2,8,8,16,128]{4,3,2,1,0:T(8,128)} %param.8) | copy-start | bytes 3145732
  1.7 16.2 %collective-permute-start = (f32[2,8,1,16,128]{4,3,2,1,0:T(8,128)S(1)}, f32[2,8,1,16,128]{4,3,2,1,0:T(8,128)S(1)}, u32[]{:S(2)}, u32[]{:S(2)}) collective-permute-start(f32[2,8,1,16,128]{4,3,2,1,0:T(8,128)S(1)} %get-tuple-element.31), channel_id=1, source_target_pairs={{0,32},{32,64},{64,96},{96,128},{128,160},{160,192},{192,224},{1,3... | collective-permute-start | bytes 393224 | tf_op jit(solution)/shard_map/ppermute | solution.py:13
  6.2 11.8 %collective-permute-start.1 = (f32[2,8,1,16,128]{4,3,2,1,0:T(8,128)S(1)}, f32[2,8,1,16,128]{4,3,2,1,0:T(8,128)S(1)}, u32[]{:S(2)}, u32[]{:S(2)}) collective-permute-start(f32[2,8,1,16,128]{4,3,2,1,0:T(8,128)S(1)} %get-tuple-element.30), channel_id=1, source_target_pairs={{32,0},{64,32},{96,64},{128,96},{160,128},{192,160},{224,192},{33,... | collective-permute-start | bytes 393224 | tf_op jit(solution)/shard_map/ppermute | solution.py:16
  18.2 5.0 %collective-permute-start.2 = (f32[2,8,10,1,128]{4,3,2,1,0:T(1,128)S(1)}, f32[2,8,10,1,128]{4,3,2,1,0:T(1,128)S(1)}, u32[]{:S(2)}, u32[]{:S(2)}) collective-permute-start(f32[2,8,10,1,128]{4,3,2,1,0:T(1,128)S(1)} %get-tuple-element.22), channel_id=1, source_target_pairs={{0,1},{1,2},{2,3},{3,4},{4,5},{5,6},{6,7},{7,8},{8,9},{9,10},{10,1... | collective-permute-start | bytes 245768 | tf_op jit(solution)/shard_map/ppermute | solution.py:13
  21.8 5.4 %collective-permute-start.3 = (f32[2,8,10,1,128]{4,3,2,1,0:T(1,128)S(1)}, f32[2,8,10,1,128]{4,3,2,1,0:T(1,128)S(1)}, u32[]{:S(2)}, u32[]{:S(2)}) collective-permute-start(f32[2,8,10,1,128]{4,3,2,1,0:T(1,128)S(1)} %get-tuple-element.23), channel_id=1, source_target_pairs={{1,0},{2,1},{3,2},{4,3},{5,4},{6,5},{7,6},{8,7},{9,8},{10,9},{11,1... | collective-permute-start | bytes 245768 | tf_op jit(solution)/shard_map/ppermute | solution.py:16
  23.2 3.9 %copy-start.6 = (f32[2,8,10,1,128]{4,3,2,1,0:T(1,128)}, f32[2,8,10,1,128]{4,3,2,1,0:T(1,128)S(1)}, u32[]{:S(2)}) copy-start(f32[2,8,10,1,128]{4,3,2,1,0:T(1,128)S(1)} %collective-permute-done.2) | copy-start | bytes 245764
  27.1 0.6 copy-start.7
  29.5 5.7 %copy-start.3 = (f32[8,16,128]{2,1,0:T(8,128)S(1)}, f32[8,16,128]{2,1,0:T(8,128)}, u32[]{:S(2)}) copy-start(f32[8,16,128]{2,1,0:T(8,128)} %param.11) | copy-start | bytes 196612
  29.5 5.7 %copy-start.4 = (f32[8,16,128]{2,1,0:T(8,128)S(1)}, f32[8,16,128]{2,1,0:T(8,128)}, u32[]{:S(2)}) copy-start(f32[8,16,128]{2,1,0:T(8,128)} %param.10) | copy-start | bytes 196612
  35.2 1.5 copy-start.5
  87.1 2.9 copy-start.8
  94.9 45.4 %all-to-all-start = ((f32[256,1,512]{2,1,0:T(1,128)}), f32[256,1,512]{2,1,0:T(1,128)S(1)}, u32[]{:S(2)}, u32[]{:S(2)}) async-start(f32[256,1,512]{2,1,0:T(1,128)} %reshape.278), calls=%async_computation | async-start | bytes 1048576 | tf_op jit(solution)/shard_map/all_to_all | solution.py:119
  149.8 4.5 %copy-start.1 = (f32[2,32,8192]{2,1,0:T(8,128)S(1)}, f32[2,32,8192]{2,1,0:T(8,128)}, u32[]{:S(2)}) copy-start(f32[2,32,8192]{2,1,0:T(8,128)} %param.12) | copy-start | bytes 6291460
  201.4 1.1 copy-start.2
  202.6 16.4 %collective-permute-start.4 = (f32[2,8,1,16,128]{4,3,2,1,0:T(8,128)S(1)}, f32[2,8,1,16,128]{4,3,2,1,0:T(8,128)S(1)}, u32[]{:S(2)}, u32[]{:S(2)}) collective-permute-start(f32[2,8,1,16,128]{4,3,2,1,0:T(8,128)S(1)} %get-tuple-element.28), channel_id=1, source_target_pairs={{0,32},{32,64},{64,96},{96,128},{128,160},{160,192},{192,224},{1,3... | collective-permute-start | bytes 393224 | tf_op jit(solution)/shard_map/ppermute | solution.py:13
  217.1 6.3 %collective-permute-start.5 = (f32[2,8,1,16,128]{4,3,2,1,0:T(8,128)S(1)}, f32[2,8,1,16,128]{4,3,2,1,0:T(8,128)S(1)}, u32[]{:S(2)}, u32[]{:S(2)}) collective-permute-start(f32[2,8,1,16,128]{4,3,2,1,0:T(8,128)S(1)} %get-tuple-element.29), channel_id=1, source_target_pairs={{32,0},{64,32},{96,64},{128,96},{160,128},{192,160},{224,192},{33,... | collective-permute-start | bytes 393224 | tf_op jit(solution)/shard_map/ppermute | solution.py:16
  223.5 4.6 %collective-permute-start.6 = (f32[2,8,10,1,128]{4,3,2,1,0:T(1,128)S(1)}, f32[2,8,10,1,128]{4,3,2,1,0:T(1,128)S(1)}, u32[]{:S(2)}, u32[]{:S(2)}) collective-permute-start(f32[2,8,10,1,128]{4,3,2,1,0:T(1,128)S(1)} %get-tuple-element.20), channel_id=1, source_target_pairs={{0,1},{1,2},{2,3},{3,4},{4,5},{5,6},{6,7},{7,8},{8,9},{9,10},{10,1... | collective-permute-start | bytes 245768 | tf_op jit(solution)/shard_map/ppermute | solution.py:13
  226.6 5.2 %collective-permute-start.7 = (f32[2,8,10,1,128]{4,3,2,1,0:T(1,128)S(1)}, f32[2,8,10,1,128]{4,3,2,1,0:T(1,128)S(1)}, u32[]{:S(2)}, u32[]{:S(2)}) collective-permute-start(f32[2,8,10,1,128]{4,3,2,1,0:T(1,128)S(1)} %get-tuple-element.21), channel_id=1, source_target_pairs={{1,0},{2,1},{3,2},{4,3},{5,4},{6,5},{7,6},{8,7},{9,8},{10,9},{11,1... | collective-permute-start | bytes 245768 | tf_op jit(solution)/shard_map/ppermute | solution.py:16
